TPU v7x, 512 devices: a whole 4x8x8 slice. The times are simulated.
512 devices in a mesh: ctx: 32 (over z, y_lo), tp: 16 (over x, y_hi, core).
Axes of the slice: x: 4, y: 8 (y_hi: 2, y_lo: 4; y = y_hi * 4 + y_lo), z: 8, core: 2. Of those that a mesh axis runs over, the one named last changes fastest.
Arguments:
- queries: bfloat16 [4096, 6144], P('ctx', 'tp'), may hold values from -6 to 6
- keys: bfloat16 [4096, 6144], P('ctx', 'tp'), may hold values from -6 to 6
- values: bfloat16 [4096, 6144], P('ctx', 'tp'), may hold values from -6 to 6
- norm_gain: float32 [6144], P('tp'), may hold values from 0.1 to 1.9
- out_weight: bfloat16 [6144, 6144], P('tp', 'ctx'), may hold values from -0.15625 to 0.15625
Outputs:
- projected: bfloat16 [4096, 6144], P('ctx', 'tp')
All inputs are finite; a program needn't handle non-finite values.
Results may differ from a plain program's by a relative error of at most 0.017.
Values may be sent and summed in bfloat16 or wider, within the bound.
A program may use at most 64 MiB of HBM per device.

v0:
```python
import jax
import jax.numpy as jnp
from jax import lax
from jax.sharding import PartitionSpec as P

HS = 128


def prefix(x, axis, combine, identity):
    count, index = (lax.axis_size(axis), lax.axis_index(axis))
    everything = lax.all_gather(x.astype(jnp.bfloat16), axis)
    start = jnp.broadcast_to(jnp.asarray(identity, x.dtype), x.shape)

    def step(k, before):
        reached = k < index
        new = combine(before, everything[k].astype(x.dtype))
        return jnp.where(reached, new, before)

    return lax.fori_loop(0, count, step, start)


def add_states(earlier, later):
    return earlier + later


def carried_state(local_state):
    return prefix(local_state, "ctx", add_states, jnp.zeros_like(local_state))


def body(queries, keys, values, norm_gain, out_weight):
    tokens_here = queries.shape[0]
    features = queries.shape[1]
    heads_here = features // HS
    query_heads = queries.reshape(tokens_here, heads_here, HS)
    key_heads = keys.reshape(tokens_here, heads_here, HS)
    value_heads = values.reshape(tokens_here, heads_here, HS)
    local_state = jnp.einsum(
        "shd,she->hde", key_heads, value_heads, preferred_element_type=jnp.float32
    )
    scores = jnp.einsum("thd,shd->hts", query_heads, key_heads, preferred_element_type=jnp.float32)
    rows_index = lax.broadcasted_iota(jnp.int32, (tokens_here, tokens_here), 0)
    cols_index = lax.broadcasted_iota(jnp.int32, (tokens_here, tokens_here), 1)
    causal = rows_index >= cols_index
    scores = jnp.where(causal[None], scores, jnp.float32(0.0)).astype(jnp.bfloat16)
    within = jnp.einsum("hts,shd->thd", scores, value_heads, preferred_element_type=jnp.float32)
    prefix_state = carried_state(local_state)
    carried = jnp.einsum(
        "thd,hde->the",
        query_heads.astype(jnp.float32),
        prefix_state,
        precision=lax.Precision.HIGHEST,
    )
    mixed_sum = within + carried
    inverse_rms = lax.rsqrt(jnp.mean(mixed_sum * mixed_sum, axis=-1, keepdims=True) + 1e-06)
    attended = (mixed_sum * inverse_rms * norm_gain.reshape(heads_here, HS)).astype(jnp.bfloat16)
    attended = attended.reshape(tokens_here, features)
    partials = jnp.dot(
        attended,
        lax.all_gather(out_weight, "ctx", axis=1, tiled=True),
        preferred_element_type=jnp.float32,
    )
    return lax.psum_scatter(partials.astype(jnp.bfloat16), "tp", scatter_dimension=1, tiled=True)


def solution(mesh):
    return jax.shard_map(
        body,
        mesh=mesh,
        in_specs=(P("ctx", "tp"), P("ctx", "tp"), P("ctx", "tp"), P("tp"), P("tp", "ctx")),
        out_specs=P("ctx", "tp"),
        check_vma=False,
    )
```

profile of v0, /device:TPU:1, one launch (start us, length us, event | category | flops | bytes accessed | tf_op | source)
XLA Modules:
  0.0 449.1 jit_solution(4256987266796342964)
XLA Ops:
  6.5 0.0 copy-start
  6.5 0.0 all-gather.6.cloned.1.call-start
  6.5 1.0 copy.18
  7.6 1.0 copy.21
  8.6 0.8 convolution_convert_fusion.1
  9.4 0.0 all-gather.6.cloned.1.call-update
  9.4 0.0 all-gather.4.cloned.1.call-start
  9.5 0.7 all-gather.4.cloned.1.call-update
  10.2 0.0 reduce-scatter.4.cloned.1.call-start
  10.3 1.0 copy.17
  11.3 0.4 convolution_bitcast_fusion.1
  11.7 146.4 %all-gather.6.cloned.1.call-done = bf16[96,128,128]{2,1,0:T(8,128)(2,1)} async-done(((bf16[3,128,128]{2,1,0:T(8,128)(2,1)}), bf16[96,128,128]{2,1,0:T(8,128)(2,1)}) %all-gather.6.cloned.1.call-update) | async-done | bytes 3145744 | tf_op jit(solution)/shard_map/all_gather | solution.py:11
  158.1 32.3 %while.14 = (s32[]{:T(128)}, f32[3,128,128]{2,1,0:T(8,128)S(1)}, s32[]{:T(128)}, bf16[32,3,128,128]{3,2,1,0:T(8,128)(2,1)}, s32[]{:T(128)}, /*index=5*/s32[]{:T(128)}) while((s32[]{:T(128)}, f32[3,128,128]{2,1,0:T(8,128)S(1)}, s32[]{:T(128)}, bf16[32,3,128,128]{3,2,1,0:T(8,128)(2,1)}, s32[]{:T(128)}, /*index=5*/s32[]{:T(128)}) %tuple.42), condition=%wide.region_1.2_spmd.clone, body=%wide.region_0.1_spmd.clone.sunk | while | flops 196612 | bytes 491613 | solution.py:19
  158.1 1.0 add_select_fusion.2
  159.1 1.0 add_select_fusion.2
  160.1 1.0 add_select_fusion.2
  161.2 1.0 add_select_fusion.2
  162.2 1.0 add_select_fusion.2
  163.2 1.0 add_select_fusion.2
  164.2 1.0 add_select_fusion.2
  165.2 1.0 add_select_fusion.2
  166.2 1.0 add_select_fusion.2
  167.2 1.0 add_select_fusion.2
  168.2 1.0 add_select_fusion.2
  169.2 1.0 add_select_fusion.2
  170.2 1.0 add_select_fusion.2
  171.2 1.0 add_select_fusion.2
  172.3 1.0 add_select_fusion.2
  173.3 1.0 add_select_fusion.2
  174.3 1.0 add_select_fusion.2
  175.3 1.0 add_select_fusion.2
  176.3 1.0 add_select_fusion.2
  177.3 1.0 add_select_fusion.2
  178.3 1.0 add_select_fusion.2
  179.3 1.0 add_select_fusion.2
  180.3 1.0 add_select_fusion.2
  181.3 1.0 add_select_fusion.2
  182.3 1.0 add_select_fusion.2
  183.4 1.0 add_select_fusion.2
  184.4 1.0 add_select_fusion.2
  185.4 1.0 add_select_fusion.2
  186.4 1.0 add_select_fusion.2
  187.4 1.0 add_select_fusion.2
  188.4 1.0 add_select_fusion.2
  189.4 1.0 add_select_fusion.2
  190.4 0.4 multiply_reduce_fusion
  190.8 0.0 copy-done
  190.8 0.1 multiply_convert_fusion
  190.9 136.9 %all-gather.4.cloned.1.call-done = bf16[384,6144]{0,1:T(8,128)(2,1)} async-done(((bf16[384,192]{0,1:T(8,128)(2,1)}), bf16[384,6144]{0,1:T(8,128)(2,1)}) %all-gather.4.cloned.1.call-update) | async-done | bytes 4718608 | tf_op jit(solution)/shard_map/all_gather | solution.py:59
  327.8 4.0 convolution_convert_fusion
  331.8 1.6 copy.30
  333.4 0.0 reduce-scatter.4.cloned.1.call-update
  333.4 107.5 %reduce-scatter.4.cloned.1.call-done = bf16[384,128]{1,0:T(8,128)(2,1)} async-done(((bf16[6144,128]{1,0:T(8,128)(2,1)}), bf16[384,128]{1,0:T(8,128)(2,1)}) %reduce-scatter.4.cloned.1.call-update) | async-done | bytes 98320
  440.9 1.6 copy.31
  (3 shorter events, 0.0 us)
Async XLA Ops:
  6.5 184.3 %copy-start = (f32[384]{0:T(512)S(1)}, f32[384]{0:T(512)}, u32[]{:S(2)}) copy-start(f32[384]{0:T(512)} %param.10) | copy-start | bytes 4612
  6.5 151.6 %all-gather.6.cloned.1.call-start = ((), (), s32[]{:S(2)}) async-start(), calls=%async_computation.2 | async-start | bytes 3244032 | tf_op jit(solution)/shard_map/all_gather | solution.py:11
  9.4 318.4 %all-gather.4.cloned.1.call-start = ((), (), s32[]{:S(2)}) async-start(), calls=%async_computation.1 | async-start | bytes 4866048 | tf_op jit(solution)/shard_map/all_gather | solution.py:59
  10.2 430.7 %reduce-scatter.4.cloned.1.call-start = ((), (), s32[]{:S(2)}) async-start(), calls=%async_computation.3 | async-start | bytes 1671168
Sparse Core Ops, SparseCore 0:
  9.6 148.5 all-gather.5
  160.2 167.5 all-gather.3
  333.5 107.3 reduce-scatter.3
where the time goes:
time: 451 us; the launch traced here: 449 us
  waiting for transfers between devices  392 us (87%)
  other arithmetic  31.7 us (7%)
  between operations  13.2 us (3%)
  local copies, waits for them, and re-layouts  6.25 us (1%)
  matrix products  5.55 us (1%)
    all_gather x1, waiting for transfers between devices, prefix(): everything = lax.all_gather(x.astype(jnp.bfloat16), axis)  146 us
    all_gather x1, waiting for transfers between devices, body(): lax.all_gather(out_weight, 'ctx', axis=1, tiled=True)  137 us
    unnamed x4, waiting for transfers between devices  108 us
    select_n x32, other arithmetic, step(): return jnp.where(reached, new, before)  31.6 us
  transfers between devices with their start and end apart: 3, of which 3 were waited for; matrix products, arithmetic and copies ran while one was open for 7% of the time, Pallas kernels for 0%

commit v1 on v0

v1 whole, which is shorter than its diff:
```python
import jax
import jax.numpy as jnp
from jax import lax
from jax.experimental import pallas as pl
from jax.experimental.pallas import tpu as pltpu
from jax.sharding import PartitionSpec as P

HS = 128
HEADS = 3
F32 = jnp.float32
BF16 = jnp.bfloat16
MESH = pl.DeviceIdType.MESH


def remote(src, dst, send, recv, device):
    return pltpu.make_async_remote_copy(
        src_ref=src, dst_ref=dst, send_sem=send, recv_sem=recv, device_id=device, device_id_type=MESH
    )


class Ring:
    def __init__(self, buf, slot, pos, device, send, recv):
        self.buf, self.slot, self.pos, self.device = buf, slot, pos, device
        self.send, self.recv = send, recv
        self.half = buf.shape[1] // 2

    def copy(self, way, step, sub, back):
        origin = lax.rem(self.pos + (8 - back if way == 0 else back), 8)
        ref = self.buf.at[self.slot(origin), pl.ds(sub * self.half, self.half)]
        i = way * 8 + (step - 1) * 2 + sub
        return remote(ref, ref, self.send.at[i], self.recv.at[i], self.device(way))

    def subs(self, way, step):
        return (0, 1) if step < 4 else (way,)

    def start(self):
        for sub in (0, 1):
            for way in (0, 1):
                self.copy(way, 1, sub, 0).start()

    def hop(self, step):
        for sub in (0, 1):
            for way in (0, 1):
                if sub in self.subs(way, step):
                    self.copy(way, step, sub, step).wait_recv()
                    if step < 4 and sub in self.subs(way, step + 1):
                        self.copy(way, step + 1, sub, step).start()

    def finish(self):
        for step in (1, 2, 3, 4):
            for way in (0, 1):
                for sub in self.subs(way, step):
                    self.copy(way, step, sub, step - 1).wait_send()


def nt(a, b):
    return lax.dot_general(a, b, (((1,), (1,)), ((), ())), preferred_element_type=F32)


def kernel(
    q_ref, k_ref, v_ref, g_ref, w_ref, o_ref,
    sq, ra, tot, rb, base, pfx, rc, within, att, wst, wt, pc_out, pc_in, px_out, px_in, f_acc, f_out, f_in,
    s1, r1, s2, r2, s3, r3, s4, r4, ws, wr, as_, ar, cs, cr, xs, xr, fs, fr,
):
    c, g = lax.axis_index("ctx"), lax.axis_index("tp")
    z, yl = lax.div(c, 4), lax.rem(c, 4)
    x, yh, core = lax.div(g, 4), lax.rem(lax.div(g, 2), 2), lax.rem(g, 2)
    y = yh * 4 + yl

    def dev(z=z, yl=yl, x=x, yh=yh, core=core):
        return (z * 4 + yl, x * 4 + yh * 2 + core)

    def dev_y(yy):
        yy = lax.rem(yy, 8)
        return dev(yl=lax.rem(yy, 4), yh=lax.div(yy, 4))

    z_swap = z + 1 - 2 * lax.rem(z, 2)
    swap_dev = dev(z=z_swap, yh=1 - yh)
    peers = [dev(yl=lax.rem(yl + d, 4), core=lax.rem(core + e, 2)) for d in range(4) for e in range(2) if d + e]
    peers += [dev(z=lax.rem(z + d, 8)) for d in range(1, 8)]
    peers += [dev_y(y + 1), dev_y(y + 7)]
    peers += [dev(x=lax.rem(x + d, 4)) for d in range(1, 4)]
    peers += [swap_dev]
    barrier = pltpu.get_barrier_semaphore()
    for peer in peers:
        pl.semaphore_signal(barrier, inc=1, device_id=peer, device_id_type=MESH)

    for h in range(HEADS):
        cols = slice(h * HS, (h + 1) * HS)
        state = lax.dot_general(
            k_ref[:, cols], v_ref[:, cols], (((0,), (0,)), ((), ())), preferred_element_type=F32
        )
        sq[cols, :] = state.astype(BF16)
    pl.semaphore_wait(barrier, len(peers))

    def quarter(i):
        return pl.ds(pl.multiple_of(i * 96, 96), 96)

    def send1(d):
        to = lax.rem(yl + d, 4)
        return remote(sq.at[quarter(to)], ra.at[yl], s1.at[d - 1], r1.at[d - 1], dev(yl=to))

    for d in (1, 2, 3):
        send1(d).start()
    ra[yl] = sq[quarter(yl), :]

    def w_slot(s):
        return lax.rem(s, 2) * 4 + lax.div(s, 2)

    wst[...] = jnp.transpose(w_ref[...])
    same = lax.rem(z, 2) == yh
    swap = remote(wst, wt.at[w_slot(z_swap)], s4.at[0], r4.at[0], swap_dev)

    def recv1(d):
        frm = lax.rem(yl + 4 - d, 4)
        return remote(sq.at[quarter(yl)], ra.at[frm], s1.at[d - 1], r1.at[d - 1], dev(yl=frm))

    for d in (1, 2, 3):
        recv1(d).wait_recv()
    tot[...] = (
        (ra[0].astype(F32) + ra[1].astype(F32)) + (ra[2].astype(F32) + ra[3].astype(F32))
    ).astype(BF16)

    def copy2(d, to):
        return remote(tot, rb.at[d - 1], s2.at[d - 1], r2.at[d - 1], dev(z=to))

    for d in range(1, 8):
        @pl.when(z + d < 8)
        def _(d=d):
            copy2(d, lax.rem(z + d, 8)).start()

    @pl.when(jnp.logical_not(same))
    def _():
        swap.start()

    @pl.when(same)
    def _():
        wt[w_slot(z)] = wst[...]

    rows = lax.broadcasted_iota(jnp.int32, (HS, HS), 0)
    columns = lax.broadcasted_iota(jnp.int32, (HS, HS), 1)
    for h in range(HEADS):
        cols = slice(h * HS, (h + 1) * HS)
        scores = jnp.where(rows >= columns, nt(q_ref[:, cols], k_ref[:, cols]), 0.0).astype(BF16)
        within[:, cols] = jnp.dot(scores, v_ref[:, cols], preferred_element_type=F32)

    base[...] = jnp.zeros_like(base)
    for d in range(1, 8):
        @pl.when(z >= d)
        def _(d=d):
            copy2(d, lax.rem(z + 8 - d, 8)).wait_recv()
            base[...] += rb[d - 1].astype(F32)
    running = base[...]
    for i in range(4):
        pfx[i] = running.astype(BF16)
        if i < 3:
            running = running + ra[i].astype(F32)

    def send3(d):
        to = lax.rem(yl + d, 4)
        return remote(pfx.at[to], rc.at[quarter(yl)], s3.at[d - 1], r3.at[d - 1], dev(yl=to))

    for d in (1, 2, 3):
        send3(d).start()
    rc[quarter(yl), :] = pfx[yl]

    w_ring = Ring(wt, w_slot, z, lambda way: dev(z=lax.rem(z + (1 if way == 0 else 7), 8)), ws, wr)

    @pl.when(jnp.logical_not(same))
    def _():
        remote(wst, wt.at[w_slot(z)], s4.at[0], r4.at[0], swap_dev).wait_recv()

    w_ring.start()

    def recv3(d):
        frm = lax.rem(yl + 4 - d, 4)
        return remote(pfx.at[yl], rc.at[quarter(frm)], s3.at[d - 1], r3.at[d - 1], dev(yl=frm))

    for d in (1, 2, 3):
        recv3(d).wait_recv()

    for h in range(HEADS):
        cols = slice(h * HS, (h + 1) * HS)
        mixed = within[:, cols] + jnp.dot(q_ref[:, cols], rc[cols, :], preferred_element_type=F32)
        scale = lax.rsqrt(jnp.mean(mixed * mixed, axis=-1, keepdims=True) + 1e-06)
        att[y, :, cols] = (mixed * scale * g_ref[:, cols]).astype(BF16)

    a_ring = Ring(att, lambda s: s, y, lambda way: dev_y(y + (1 if way == 0 else 7)), as_, ar)
    a_ring.start()
    w_ring.hop(1)
    a_ring.hop(1)
    w_ring.hop(2)
    a_ring.hop(2)
    w_ring.hop(3)
    a_ring.hop(3)
    a_ring.hop(4)
    w_ring.hop(4)

    def tokens(p, half):
        return att[pl.ds(p * 4 + 2 * half, 2)].reshape(2 * HS, HEADS * HS)

    def unit(i, a):
        m = lax.rem(x + i, 4)
        return nt(wt[m], a[0]) + nt(wt[4 + m], a[1])

    partner = dev(core=1 - core)

    def copy_c(i):
        return remote(pc_out.at[i - 1], pc_in.at[i - 1], cs.at[i - 1], cr.at[i - 1], partner)

    theirs = (tokens(0, 1 - core), tokens(1, 1 - core))
    for i in (1, 2, 3, 4):
        pc_out[i - 1] = unit(i, theirs).astype(BF16)
        copy_c(i).start()

    def copy_x(i, to):
        return remote(px_out.at[i - 1], px_in.at[i - 1], xs.at[i - 1], xr.at[i - 1], dev(x=to))

    ours = (tokens(0, core), tokens(1, core))
    for i in (1, 2, 3, 4):
        mine = unit(i, ours)
        copy_c(i).wait_recv()
        mine = mine + pc_in[i - 1].astype(F32)
        if i < 4:
            px_out[i - 1] = mine.astype(BF16)
            copy_x(i, lax.rem(x + i, 4)).start()
        else:
            f_acc[...] = mine
    for i in (1, 2, 3):
        copy_x(i, lax.rem(x + 4 - i, 4)).wait_recv()
    total = f_acc[...] + px_in[0].astype(F32) + px_in[1].astype(F32) + px_in[2].astype(F32)

    f_out[0] = total[:, :HS].astype(BF16)
    f_out[1] = total[:, HS:].astype(BF16)
    half = lax.rem(yl, 2)

    def copy_f(i):
        return remote(
            f_out.at[i], f_in.at[half], fs.at[i], fr.at[half], dev(yl=2 * core + i, core=lax.div(yl, 2))
        )

    for i in (0, 1):
        @pl.when(2 * core + i != yl)
        def _(i=i):
            copy_f(i).start()

        @pl.when(2 * core + i == yl)
        def _(i=i):
            f_in[i] = f_out[i]

    for i in (0, 1):
        @pl.when(2 * core + i != yl)
        def _(i=i):
            remote(
                f_out.at[i], f_in.at[i], fs.at[i], fr.at[i], dev(yl=2 * core + i, core=lax.div(yl, 2))
            ).wait_recv()

    o_ref[...] = jnp.transpose(f_in[...].reshape(HEADS * HS, HS))

    for d in (1, 2, 3):
        send1(d).wait_send()
        send3(d).wait_send()
        copy_x(d, lax.rem(x + d, 4)).wait_send()
    for d in range(1, 8):
        @pl.when(z + d < 8)
        def _(d=d):
            copy2(d, lax.rem(z + d, 8)).wait_send()

    @pl.when(jnp.logical_not(same))
    def _():
        swap.wait_send()

    w_ring.finish()
    a_ring.finish()
    for i in (1, 2, 3, 4):
        copy_c(i).wait_send()
    for i in (0, 1):
        @pl.when(2 * core + i != yl)
        def _(i=i):
            copy_f(i).wait_send()


def body(queries, keys, values, norm_gain, out_weight):
    dma = [pltpu.SemaphoreType.DMA((n,)) for n in (3, 7, 3, 1, 16, 16, 4, 3, 2) for _ in (0, 1)]
    return pl.pallas_call(
        kernel,
        out_shape=jax.ShapeDtypeStruct((HS, HEADS * HS), BF16),
        in_specs=[pl.BlockSpec(memory_space=pltpu.VMEM)] * 5,
        out_specs=pl.BlockSpec(memory_space=pltpu.VMEM),
        scratch_shapes=[
            pltpu.VMEM((384, 128), BF16),
            pltpu.VMEM((4, 96, 128), BF16),
            pltpu.VMEM((96, 128), BF16),
            pltpu.VMEM((7, 96, 128), BF16),
            pltpu.VMEM((96, 128), F32),
            pltpu.VMEM((4, 96, 128), BF16),
            pltpu.VMEM((384, 128), BF16),
            pltpu.VMEM((128, 384), F32),
            pltpu.VMEM((8, 128, 384), BF16),
            pltpu.VMEM((192, 384), BF16),
            pltpu.VMEM((8, 192, 384), BF16),
            pltpu.VMEM((4, 192, 256), BF16),
            pltpu.VMEM((4, 192, 256), BF16),
            pltpu.VMEM((3, 192, 256), BF16),
            pltpu.VMEM((3, 192, 256), BF16),
            pltpu.VMEM((192, 256), F32),
            pltpu.VMEM((2, 192, 128), BF16),
            pltpu.VMEM((2, 192, 128), BF16),
        ] + dma,
        compiler_params=pltpu.CompilerParams(collective_id=0, has_side_effects=True),
    )(queries, keys, values, norm_gain.reshape(1, HEADS * HS), out_weight)


def solution(mesh):
    return jax.shard_map(
        body,
        mesh=mesh,
        in_specs=(P("ctx", "tp"), P("ctx", "tp"), P("ctx", "tp"), P("tp"), P("tp", "ctx")),
        out_specs=P("ctx", "tp"),
        check_vma=False,
    )
```

time: 451 us -> 67 us (0.15)
  waiting for transfers between devices: 392 us -> 0 us
  Pallas kernels: 0 us -> 62.2 us
  other arithmetic: 31.7 us -> 0 us
  between operations: 13.2 us -> 0.01 us
  matrix products: 5.55 us -> 0 us
    all_gather x2 -> x0, waiting for transfers between devices: 283 us -> none  [the longest x1 146 us: prefix(): everything = lax.all_gather(x.astype(jnp.bfloat16), axis)]
    unnamed x4 -> x0, waiting for transfers between devices: 108 us -> none
    pallas_call x0 -> x1, Pallas kernels: none -> 62.2 us  [body(): pl.pallas_call(kernel, out_shape=jax.ShapeDtypeStruct((HS, HEADS * HS), B...]
    select_n x32 -> x0, other arithmetic: 31.6 us -> none  [step(): return jnp.where(reached, new, before)]
    dot_general x4 -> x0, matrix products: 5.55 us -> none  [the longest x1 3.95 us: body(): jnp.dot(attended, lax.all_gather(out_weight, 'ctx', axis=1, tiled=True),...]
  transfers between devices with their start and end apart: 3 -> 0, of which waited for: 3 -> 0; matrix products, arithmetic and copies ran while one was open for 7% -> 0% of each run, Pallas kernels for 0% -> 0%
where the time goes in v1:
time: 67 us; the launch traced here: 66.8 us
  Pallas kernels  62.2 us (93%)
  local copies, waits for them, and re-layouts  4.51 us (7%)
    pallas_call x1, Pallas kernels, body(): pl.pallas_call(kernel, out_shape=jax.ShapeDtypeStruct((HS, HEADS * HS), B...  62.2 us
    unnamed x2, local copies, waits for them, and re-layouts  3.26 us

profile of v1, /device:TPU:1, one launch (start us, length us, event | category | flops | bytes accessed | tf_op | source)
XLA Modules:
  0.0 66.8 jit_solution(14130888123919195604)
XLA Ops:
  0.0 1.2 %reshape.3.g_ref = f32[1,384]{1,0:T(1,128)} reshape(f32[384]{0:T(512)} %param.8) | data formatting | bytes 3072 | tf_op jit(solution)/shard_map/reshape | solution.py:311
  1.2 1.7 %copy.6.w_ref = bf16[384,192]{1,0:T(8,128)(2,1)} copy(bf16[384,192]{0,1:T(8,128)(2,1)} %param.9) | data formatting | bytes 294912 | tf_op args[4]
  3.0 62.2 %shard_map.55 = bf16[128,384]{1,0:T(8,128)(2,1)} custom-call(bf16[128,384]{1,0:T(8,128)(2,1)} %q_ref.1, bf16[128,384]{1,0:T(8,128)(2,1)} %k_ref.1, bf16[128,384]{1,0:T(8,128)(2,1)} %v_ref.1, f32[1,384]{1,0:T(1,128)} %reshape.3.g_ref, bf16[384,192]{1,0:T(8,128)(2,1)} %copy.6.w_ref), custom_call_target="tpu_custom_call" | custom-call | tf_op jit(solution)/shard_map/pallas_call | solution.py:285
  65.2 1.5 %copy.8 = bf16[128,384]{1,0:T(8,128)(2,1)} copy(bf16[128,384]{1,0:T(8,128)(2,1)} %shard_map.55) | data formatting | bytes 196608

commit v2 on v1

--- a/solution.py
+++ b/solution.py
@@ -59,7 +59,7 @@
 
 def kernel(
     q_ref, k_ref, v_ref, g_ref, w_ref, o_ref,
-    sq, ra, tot, rb, base, pfx, rc, within, att, wst, wt, pc_out, pc_in, px_out, px_in, f_acc, f_out, f_in,
+    sq, ra, tot, rb, base, pfx, rc, within, att, wt, pc_out, pc_in, px_out, px_in, f_acc, f_out, f_in,
     s1, r1, s2, r2, s3, r3, s4, r4, ws, wr, as_, ar, cs, cr, xs, xr, fs, fr,
 ):
     c, g = lax.axis_index("ctx"), lax.axis_index("tp")
@@ -107,9 +107,16 @@
     def w_slot(s):
         return lax.rem(s, 2) * 4 + lax.div(s, 2)
 
-    wst[...] = jnp.transpose(w_ref[...])
     same = lax.rem(z, 2) == yh
-    swap = remote(wst, wt.at[w_slot(z_swap)], s4.at[0], r4.at[0], swap_dev)
+    swap = remote(w_ref, wt.at[w_slot(z_swap)], s4.at[0], r4.at[0], swap_dev)
+
+    @pl.when(jnp.logical_not(same))
+    def _():
+        swap.start()
+
+    @pl.when(same)
+    def _():
+        wt[w_slot(z)] = w_ref[...]
 
     def recv1(d):
         frm = lax.rem(yl + 4 - d, 4)
@@ -128,14 +135,6 @@
         @pl.when(z + d < 8)
         def _(d=d):
             copy2(d, lax.rem(z + d, 8)).start()
-
-    @pl.when(jnp.logical_not(same))
-    def _():
-        swap.start()
-
-    @pl.when(same)
-    def _():
-        wt[w_slot(z)] = wst[...]
 
     rows = lax.broadcasted_iota(jnp.int32, (HS, HS), 0)
     columns = lax.broadcasted_iota(jnp.int32, (HS, HS), 1)
@@ -168,7 +167,7 @@
 
     @pl.when(jnp.logical_not(same))
     def _():
-        remote(wst, wt.at[w_slot(z)], s4.at[0], r4.at[0], swap_dev).wait_recv()
+        remote(w_ref, wt.at[w_slot(z)], s4.at[0], r4.at[0], swap_dev).wait_recv()
 
     w_ring.start()
 
@@ -183,7 +182,7 @@
         cols = slice(h * HS, (h + 1) * HS)
         mixed = within[:, cols] + jnp.dot(q_ref[:, cols], rc[cols, :], preferred_element_type=F32)
         scale = lax.rsqrt(jnp.mean(mixed * mixed, axis=-1, keepdims=True) + 1e-06)
-        att[y, :, cols] = (mixed * scale * g_ref[:, cols]).astype(BF16)
+        att[y, :, cols] = (mixed * scale * g_ref[cols]).astype(BF16)
 
     a_ring = Ring(att, lambda s: s, y, lambda way: dev_y(y + (1 if way == 0 else 7)), as_, ar)
     a_ring.start()
@@ -297,7 +296,6 @@
             pltpu.VMEM((384, 128), BF16),
             pltpu.VMEM((128, 384), F32),
             pltpu.VMEM((8, 128, 384), BF16),
-            pltpu.VMEM((192, 384), BF16),
             pltpu.VMEM((8, 192, 384), BF16),
             pltpu.VMEM((4, 192, 256), BF16),
             pltpu.VMEM((4, 192, 256), BF16),
@@ -308,7 +306,7 @@
             pltpu.VMEM((2, 192, 128), BF16),
         ] + dma,
         compiler_params=pltpu.CompilerParams(collective_id=0, has_side_effects=True),
-    )(queries, keys, values, norm_gain.reshape(1, HEADS * HS), out_weight)
+    )(queries, keys, values, norm_gain, jnp.transpose(out_weight))
 
 
 def solution(mesh):

time: 67 us -> 64 us (0.955)
  local copies, waits for them, and re-layouts: 4.51 us -> 1.54 us
    unnamed x2 -> x1, local copies, waits for them, and re-layouts: 3.26 us -> 1.54 us
    reshape x1 -> x0, local copies, waits for them, and re-layouts: 1.24 us -> none  [body(): norm_gain.reshape(1, HEADS * HS)]
where the time goes in v2:
time: 64 us; the launch traced here: 63.8 us
  Pallas kernels  62.3 us (97%)
  local copies, waits for them, and re-layouts  1.54 us (2%)
    pallas_call x1, Pallas kernels, body(): pl.pallas_call(kernel, out_shape=jax.ShapeDtypeStruct((HS, HEADS * HS), B...  62.3 us
    unnamed x1, local copies, waits for them, and re-layouts  1.54 us

profile of v2, /device:TPU:1, one launch (start us, length us, event | category | flops | bytes accessed | tf_op | source)
XLA Modules:
  0.0 63.8 jit_solution(13516153230433484165)
XLA Ops:
  0.0 62.3 %shard_map.55 = bf16[128,384]{1,0:T(8,128)(2,1)} custom-call(bf16[128,384]{1,0:T(8,128)(2,1)} %q_ref.1, bf16[128,384]{1,0:T(8,128)(2,1)} %k_ref.1, bf16[128,384]{1,0:T(8,128)(2,1)} %v_ref.1, f32[384]{0:T(512)} %g_ref.1, bf16[192,384]{1,0:T(8,128)(2,1)} %bitcast.1), custom_call_target="tpu_custom_call" | custom-call | tf_op jit(solution)/shard_map/pallas_call | solution.py:284
  62.3 1.5 %copy.7 = bf16[128,384]{1,0:T(8,128)(2,1)} copy(bf16[128,384]{1,0:T(8,128)(2,1)} %shard_map.55) | data formatting | bytes 196608

commit v3 on v2

--- a/solution.py
+++ b/solution.py
@@ -53,6 +53,50 @@
                     self.copy(way, step, sub, step - 1).wait_send()
 
 
+class Line:
+    def __init__(self, buf, pos, device, send, recv):
+        self.buf, self.pos, self.device, self.send, self.recv = buf, pos, device, send, recv
+        self.half = buf.shape[1] // 2
+
+    def copy(self, way, step, sub, back):
+        origin = lax.rem(self.pos + (4 - back if way == 0 else back), 4)
+        ref = self.buf.at[origin, pl.ds(sub * self.half, self.half)]
+        i = way * 6 + (step - 1) * 2 + sub
+        return remote(ref, ref, self.send.at[i], self.recv.at[i], self.device(way))
+
+    def room(self, way):
+        return self.pos if way == 0 else 3 - self.pos
+
+    def sends(self, way, step):
+        return jnp.logical_and(self.room(way) < 3, self.room(way) >= step - 1)
+
+    def start(self):
+        for sub in (0, 1):
+            for way in (0, 1):
+                @pl.when(self.sends(way, 1))
+                def _():
+                    self.copy(way, 1, sub, 0).start()
+
+    def hop(self, step):
+        for sub in (0, 1):
+            for way in (0, 1):
+                @pl.when(self.room(way) >= step)
+                def _():
+                    self.copy(way, step, sub, step).wait_recv()
+                if step < 3:
+                    @pl.when(self.sends(way, step + 1))
+                    def _():
+                        self.copy(way, step + 1, sub, step).start()
+
+    def finish(self):
+        for step in (1, 2, 3):
+            for way in (0, 1):
+                for sub in (0, 1):
+                    @pl.when(self.sends(way, step))
+                    def _():
+                        self.copy(way, step, sub, step - 1).wait_send()
+
+
 def nt(a, b):
     return lax.dot_general(a, b, (((1,), (1,)), ((), ())), preferred_element_type=F32)
 
@@ -60,27 +104,19 @@
 def kernel(
     q_ref, k_ref, v_ref, g_ref, w_ref, o_ref,
     sq, ra, tot, rb, base, pfx, rc, within, att, wt, pc_out, pc_in, px_out, px_in, f_acc, f_out, f_in,
-    s1, r1, s2, r2, s3, r3, s4, r4, ws, wr, as_, ar, cs, cr, xs, xr, fs, fr,
+    s1, r1, s2, r2, s3, r3, ws, wr, as_, ar, cs, cr, xs, xr, fs, fr,
 ):
     c, g = lax.axis_index("ctx"), lax.axis_index("tp")
     z, yl = lax.div(c, 4), lax.rem(c, 4)
     x, yh, core = lax.div(g, 4), lax.rem(lax.div(g, 2), 2), lax.rem(g, 2)
-    y = yh * 4 + yl
 
     def dev(z=z, yl=yl, x=x, yh=yh, core=core):
         return (z * 4 + yl, x * 4 + yh * 2 + core)
 
-    def dev_y(yy):
-        yy = lax.rem(yy, 8)
-        return dev(yl=lax.rem(yy, 4), yh=lax.div(yy, 4))
-
-    z_swap = z + 1 - 2 * lax.rem(z, 2)
-    swap_dev = dev(z=z_swap, yh=1 - yh)
     peers = [dev(yl=lax.rem(yl + d, 4), core=lax.rem(core + e, 2)) for d in range(4) for e in range(2) if d + e]
     peers += [dev(z=lax.rem(z + d, 8)) for d in range(1, 8)]
-    peers += [dev_y(y + 1), dev_y(y + 7)]
+    peers += [dev(yl=2 * core + i, yh=1 - yh, core=lax.div(yl, 2)) for i in range(2)]
     peers += [dev(x=lax.rem(x + d, 4)) for d in range(1, 4)]
-    peers += [swap_dev]
     barrier = pltpu.get_barrier_semaphore()
     for peer in peers:
         pl.semaphore_signal(barrier, inc=1, device_id=peer, device_id_type=MESH)
@@ -104,19 +140,10 @@
         send1(d).start()
     ra[yl] = sq[quarter(yl), :]
 
-    def w_slot(s):
-        return lax.rem(s, 2) * 4 + lax.div(s, 2)
-
-    same = lax.rem(z, 2) == yh
-    swap = remote(w_ref, wt.at[w_slot(z_swap)], s4.at[0], r4.at[0], swap_dev)
-
-    @pl.when(jnp.logical_not(same))
-    def _():
-        swap.start()
-
-    @pl.when(same)
-    def _():
-        wt[w_slot(z)] = w_ref[...]
+    wt[z] = w_ref[...]
+    w_ring = Ring(wt, lambda o: o, z, lambda way: dev(z=lax.rem(z + (1 if way == 0 else 7), 8)), ws, wr)
+
+    w_ring.start()
 
     def recv1(d):
         frm = lax.rem(yl + 4 - d, 4)
@@ -143,6 +170,7 @@
         scores = jnp.where(rows >= columns, nt(q_ref[:, cols], k_ref[:, cols]), 0.0).astype(BF16)
         within[:, cols] = jnp.dot(scores, v_ref[:, cols], preferred_element_type=F32)
 
+    w_ring.hop(1)
     base[...] = jnp.zeros_like(base)
     for d in range(1, 8):
         @pl.when(z >= d)
@@ -163,13 +191,7 @@
         send3(d).start()
     rc[quarter(yl), :] = pfx[yl]
 
-    w_ring = Ring(wt, w_slot, z, lambda way: dev(z=lax.rem(z + (1 if way == 0 else 7), 8)), ws, wr)
-
-    @pl.when(jnp.logical_not(same))
-    def _():
-        remote(w_ref, wt.at[w_slot(z)], s4.at[0], r4.at[0], swap_dev).wait_recv()
-
-    w_ring.start()
+    w_ring.hop(2)
 
     def recv3(d):
         frm = lax.rem(yl + 4 - d, 4)
@@ -182,41 +204,41 @@
         cols = slice(h * HS, (h + 1) * HS)
         mixed = within[:, cols] + jnp.dot(q_ref[:, cols], rc[cols, :], preferred_element_type=F32)
         scale = lax.rsqrt(jnp.mean(mixed * mixed, axis=-1, keepdims=True) + 1e-06)
-        att[y, :, cols] = (mixed * scale * g_ref[cols]).astype(BF16)
-
-    a_ring = Ring(att, lambda s: s, y, lambda way: dev_y(y + (1 if way == 0 else 7)), as_, ar)
-    a_ring.start()
-    w_ring.hop(1)
-    a_ring.hop(1)
-    w_ring.hop(2)
-    a_ring.hop(2)
+        att[yl, :, cols] = (mixed * scale * g_ref[cols]).astype(BF16)
+
+    a_line = Line(att, yl, lambda way: dev(yl=lax.rem(yl + (1 if way == 0 else 3), 4)), as_, ar)
+    a_line.start()
     w_ring.hop(3)
-    a_ring.hop(3)
-    a_ring.hop(4)
+    a_line.hop(1)
+    a_line.hop(2)
     w_ring.hop(4)
-
-    def tokens(p, half):
-        return att[pl.ds(p * 4 + 2 * half, 2)].reshape(2 * HS, HEADS * HS)
+    a_line.hop(3)
+
+    def tokens(half):
+        return att[pl.ds(2 * half, 2)].reshape(2 * HS, HEADS * HS)
 
     def unit(i, a):
-        m = lax.rem(x + i, 4)
-        return nt(wt[m], a[0]) + nt(wt[4 + m], a[1])
+        return nt(wt[pl.ds(2 * lax.rem(x + i, 4), 2)].reshape(2 * 192, HEADS * HS), a)
 
     partner = dev(core=1 - core)
 
     def copy_c(i):
         return remote(pc_out.at[i - 1], pc_in.at[i - 1], cs.at[i - 1], cr.at[i - 1], partner)
 
-    theirs = (tokens(0, 1 - core), tokens(1, 1 - core))
-    for i in (1, 2, 3, 4):
+    def copy_x(i, to):
+        return remote(px_out.at[i - 1], px_in.at[i - 1], xs.at[i - 1], xr.at[i - 1], dev(x=to))
+
+    theirs, ours = tokens(1 - core), tokens(core)
+
+    def give(i):
         pc_out[i - 1] = unit(i, theirs).astype(BF16)
         copy_c(i).start()
 
-    def copy_x(i, to):
-        return remote(px_out.at[i - 1], px_in.at[i - 1], xs.at[i - 1], xr.at[i - 1], dev(x=to))
-
-    ours = (tokens(0, core), tokens(1, core))
-    for i in (1, 2, 3, 4):
+    order = (2, 1, 3, 4)
+    give(order[0])
+    for n, i in enumerate(order):
+        if i < 4:
+            give(order[n + 1])
         mine = unit(i, ours)
         copy_c(i).wait_recv()
         mine = mine + pc_in[i - 1].astype(F32)
@@ -229,32 +251,35 @@
         copy_x(i, lax.rem(x + 4 - i, 4)).wait_recv()
     total = f_acc[...] + px_in[0].astype(F32) + px_in[1].astype(F32) + px_in[2].astype(F32)
 
-    f_out[0] = total[:, :HS].astype(BF16)
-    f_out[1] = total[:, HS:].astype(BF16)
+    f_acc[...] = total
     half = lax.rem(yl, 2)
 
-    def copy_f(i):
-        return remote(
-            f_out.at[i], f_in.at[half], fs.at[i], fr.at[half], dev(yl=2 * core + i, core=lax.div(yl, 2))
-        )
-
+    def copy_f(e, i, slot):
+        to = dev(yl=2 * core + i, yh=lax.rem(yh + e, 2), core=lax.div(yl, 2))
+        return remote(f_out.at[e * 2 + i], f_in.at[e * 2 + slot], fs.at[e * 2 + i], fr.at[e * 2 + slot], to)
+
+    def each_f(act):
+        for e in (1, 0):
+            for i in (0, 1):
+                if e:
+                    act(e, i)
+                else:
+                    pl.when(2 * core + i != yl)(lambda e=e, i=i: act(e, i))
+
+    for e in (1, 0):
+        part = f_acc[pl.ds(pl.multiple_of(lax.rem(yh + e, 2) * 192, 192), 192), :]
+        f_out[e * 2] = part[:, :HS].astype(BF16)
+        f_out[e * 2 + 1] = part[:, HS:].astype(BF16)
+    each_f(lambda e, i: copy_f(e, i, half).start())
     for i in (0, 1):
-        @pl.when(2 * core + i != yl)
-        def _(i=i):
-            copy_f(i).start()
-
         @pl.when(2 * core + i == yl)
         def _(i=i):
             f_in[i] = f_out[i]
-
-    for i in (0, 1):
-        @pl.when(2 * core + i != yl)
-        def _(i=i):
-            remote(
-                f_out.at[i], f_in.at[i], fs.at[i], fr.at[i], dev(yl=2 * core + i, core=lax.div(yl, 2))
-            ).wait_recv()
-
-    o_ref[...] = jnp.transpose(f_in[...].reshape(HEADS * HS, HS))
+    each_f(lambda e, i: copy_f(e, i, i).wait_recv())
+
+    same = f_in[0:2].reshape(HEADS * HS, HS).astype(F32)
+    other = f_in[2:4].reshape(HEADS * HS, HS).astype(F32)
+    o_ref[...] = jnp.transpose((same + other).astype(BF16))
 
     for d in (1, 2, 3):
         send1(d).wait_send()
@@ -265,22 +290,15 @@
         def _(d=d):
             copy2(d, lax.rem(z + d, 8)).wait_send()
 
-    @pl.when(jnp.logical_not(same))
-    def _():
-        swap.wait_send()
-
     w_ring.finish()
-    a_ring.finish()
+    a_line.finish()
     for i in (1, 2, 3, 4):
         copy_c(i).wait_send()
-    for i in (0, 1):
-        @pl.when(2 * core + i != yl)
-        def _(i=i):
-            copy_f(i).wait_send()
+    each_f(lambda e, i: copy_f(e, i, half).wait_send())
 
 
 def body(queries, keys, values, norm_gain, out_weight):
-    dma = [pltpu.SemaphoreType.DMA((n,)) for n in (3, 7, 3, 1, 16, 16, 4, 3, 2) for _ in (0, 1)]
+    dma = [pltpu.SemaphoreType.DMA((n,)) for n in (3, 7, 3, 16, 12, 4, 3, 4) for _ in (0, 1)]
     return pl.pallas_call(
         kernel,
         out_shape=jax.ShapeDtypeStruct((HS, HEADS * HS), BF16),
@@ -295,15 +313,15 @@
             pltpu.VMEM((4, 96, 128), BF16),
             pltpu.VMEM((384, 128), BF16),
             pltpu.VMEM((128, 384), F32),
-            pltpu.VMEM((8, 128, 384), BF16),
+            pltpu.VMEM((4, 128, 384), BF16),
             pltpu.VMEM((8, 192, 384), BF16),
-            pltpu.VMEM((4, 192, 256), BF16),
-            pltpu.VMEM((4, 192, 256), BF16),
-            pltpu.VMEM((3, 192, 256), BF16),
-            pltpu.VMEM((3, 192, 256), BF16),
-            pltpu.VMEM((192, 256), F32),
-            pltpu.VMEM((2, 192, 128), BF16),
-            pltpu.VMEM((2, 192, 128), BF16),
+            pltpu.VMEM((4, 384, 256), BF16),
+            pltpu.VMEM((4, 384, 256), BF16),
+            pltpu.VMEM((3, 384, 256), BF16),
+            pltpu.VMEM((3, 384, 256), BF16),
+            pltpu.VMEM((384, 256), F32),
+            pltpu.VMEM((4, 192, 128), BF16),
+            pltpu.VMEM((4, 192, 128), BF16),
         ] + dma,
         compiler_params=pltpu.CompilerParams(collective_id=0, has_side_effects=True),
     )(queries, keys, values, norm_gain, jnp.transpose(out_weight))

time: 64 us -> 59.9 us (0.936)
  Pallas kernels: 62.3 us -> 58.1 us
    pallas_call x1, Pallas kernels: 62.3 us -> 58.1 us  [body(): pl.pallas_call(kernel, out_shape=jax.ShapeDtypeStruct((HS, HEADS * HS), B...]
where the time goes in v3:
time: 59.9 us; the launch traced here: 59.6 us
  Pallas kernels  58.1 us (97%)
  local copies, waits for them, and re-layouts  1.54 us (3%)
    pallas_call x1, Pallas kernels, body(): pl.pallas_call(kernel, out_shape=jax.ShapeDtypeStruct((HS, HEADS * HS), B...  58.1 us
    unnamed x1, local copies, waits for them, and re-layouts  1.54 us

profile of v3, /device:TPU:1, one launch (start us, length us, event | category | flops | bytes accessed | tf_op | source)
XLA Modules:
  0.0 59.6 jit_solution(6493801882068815164)
XLA Ops:
  0.0 58.1 %shard_map.55 = bf16[128,384]{1,0:T(8,128)(2,1)} custom-call(bf16[128,384]{1,0:T(8,128)(2,1)} %q_ref.1, bf16[128,384]{1,0:T(8,128)(2,1)} %k_ref.1, bf16[128,384]{1,0:T(8,128)(2,1)} %v_ref.1, f32[384]{0:T(512)} %g_ref.1, bf16[192,384]{1,0:T(8,128)(2,1)} %bitcast.1), custom_call_target="tpu_custom_call" | custom-call | tf_op jit(solution)/shard_map/pallas_call | solution.py:302
  58.1 1.5 %copy.7 = bf16[128,384]{1,0:T(8,128)(2,1)} copy(bf16[128,384]{1,0:T(8,128)(2,1)} %shard_map.55) | data formatting | bytes 196608

commit v4 on v3

--- a/solution.py
+++ b/solution.py
@@ -217,49 +217,47 @@
     def tokens(half):
         return att[pl.ds(2 * half, 2)].reshape(2 * HS, HEADS * HS)
 
-    def unit(i, a):
-        return nt(wt[pl.ds(2 * lax.rem(x + i, 4), 2)].reshape(2 * 192, HEADS * HS), a)
+    def unit(e, i, a):
+        return nt(wt[2 * lax.rem(x + i, 4) + lax.rem(yh + e, 2)], a)
 
     partner = dev(core=1 - core)
 
-    def copy_c(i):
-        return remote(pc_out.at[i - 1], pc_in.at[i - 1], cs.at[i - 1], cr.at[i - 1], partner)
-
-    def copy_x(i, to):
-        return remote(px_out.at[i - 1], px_in.at[i - 1], xs.at[i - 1], xr.at[i - 1], dev(x=to))
+    def copy_c(e, i):
+        n = e * 4 + i - 1
+        return remote(pc_out.at[n], pc_in.at[n], cs.at[n], cr.at[n], partner)
+
+    def copy_x(e, i, to):
+        n = e * 3 + i - 1
+        return remote(px_out.at[n], px_in.at[n], xs.at[n], xr.at[n], dev(x=to))
 
     theirs, ours = tokens(1 - core), tokens(core)
 
-    def give(i):
-        pc_out[i - 1] = unit(i, theirs).astype(BF16)
-        copy_c(i).start()
-
-    order = (2, 1, 3, 4)
-    give(order[0])
-    for n, i in enumerate(order):
+    def give(e, i):
+        pc_out[e * 4 + i - 1] = unit(e, i, theirs).astype(BF16)
+        copy_c(e, i).start()
+
+    order = [(e, i) for e in (1, 0) for i in (2, 1, 3, 4)]
+    give(*order[0])
+    for n, (e, i) in enumerate(order):
+        if n < 7:
+            give(*order[n + 1])
+        mine = unit(e, i, ours)
+        copy_c(e, i).wait_recv()
+        mine = mine + pc_in[e * 4 + i - 1].astype(F32)
         if i < 4:
-            give(order[n + 1])
-        mine = unit(i, ours)
-        copy_c(i).wait_recv()
-        mine = mine + pc_in[i - 1].astype(F32)
-        if i < 4:
-            px_out[i - 1] = mine.astype(BF16)
-            copy_x(i, lax.rem(x + i, 4)).start()
+            px_out[e * 3 + i - 1] = mine.astype(BF16)
+            copy_x(e, i, lax.rem(x + i, 4)).start()
         else:
-            f_acc[...] = mine
-    for i in (1, 2, 3):
-        copy_x(i, lax.rem(x + 4 - i, 4)).wait_recv()
-    total = f_acc[...] + px_in[0].astype(F32) + px_in[1].astype(F32) + px_in[2].astype(F32)
-
-    f_acc[...] = total
+            f_acc[e] = mine
+
     half = lax.rem(yl, 2)
 
     def copy_f(e, i, slot):
         to = dev(yl=2 * core + i, yh=lax.rem(yh + e, 2), core=lax.div(yl, 2))
         return remote(f_out.at[e * 2 + i], f_in.at[e * 2 + slot], fs.at[e * 2 + i], fr.at[e * 2 + slot], to)
 
-    def each_f(act):
-        for e in (1, 0):
+    def each_f(act, es=(1, 0)):
+        for e in es:
             for i in (0, 1):
                 if e:
                     act(e, i)
@@ -267,10 +265,14 @@
                     pl.when(2 * core + i != yl)(lambda e=e, i=i: act(e, i))
 
     for e in (1, 0):
-        part = f_acc[pl.ds(pl.multiple_of(lax.rem(yh + e, 2) * 192, 192), 192), :]
-        f_out[e * 2] = part[:, :HS].astype(BF16)
-        f_out[e * 2 + 1] = part[:, HS:].astype(BF16)
-    each_f(lambda e, i: copy_f(e, i, half).start())
+        for i in (1, 2, 3):
+            copy_x(e, i, lax.rem(x + 4 - i, 4)).wait_recv()
+        total = f_acc[e]
+        for i in (1, 2, 3):
+            total = total + px_in[e * 3 + i - 1].astype(F32)
+        f_out[e * 2] = total[:, :HS].astype(BF16)
+        f_out[e * 2 + 1] = total[:, HS:].astype(BF16)
+        each_f(lambda e, i: copy_f(e, i, half).start(), (e,))
     for i in (0, 1):
         @pl.when(2 * core + i == yl)
         def _(i=i):
@@ -284,7 +286,8 @@
     for d in (1, 2, 3):
         send1(d).wait_send()
         send3(d).wait_send()
-        copy_x(d, lax.rem(x + d, 4)).wait_send()
+        copy_x(0, d, lax.rem(x + d, 4)).wait_send()
+        copy_x(1, d, lax.rem(x + d, 4)).wait_send()
     for d in range(1, 8):
         @pl.when(z + d < 8)
         def _(d=d):
@@ -293,12 +296,13 @@
     w_ring.finish()
     a_line.finish()
     for i in (1, 2, 3, 4):
-        copy_c(i).wait_send()
+        copy_c(0, i).wait_send()
+        copy_c(1, i).wait_send()
     each_f(lambda e, i: copy_f(e, i, half).wait_send())
 
 
 def body(queries, keys, values, norm_gain, out_weight):
-    dma = [pltpu.SemaphoreType.DMA((n,)) for n in (3, 7, 3, 16, 12, 4, 3, 4) for _ in (0, 1)]
+    dma = [pltpu.SemaphoreType.DMA((n,)) for n in (3, 7, 3, 16, 12, 8, 6, 4) for _ in (0, 1)]
     return pl.pallas_call(
         kernel,
         out_shape=jax.ShapeDtypeStruct((HS, HEADS * HS), BF16),
@@ -315,11 +319,11 @@
             pltpu.VMEM((128, 384), F32),
             pltpu.VMEM((4, 128, 384), BF16),
             pltpu.VMEM((8, 192, 384), BF16),
-            pltpu.VMEM((4, 384, 256), BF16),
-            pltpu.VMEM((4, 384, 256), BF16),
-            pltpu.VMEM((3, 384, 256), BF16),
-            pltpu.VMEM((3, 384, 256), BF16),
-            pltpu.VMEM((384, 256), F32),
+            pltpu.VMEM((8, 192, 256), BF16),
+            pltpu.VMEM((8, 192, 256), BF16),
+            pltpu.VMEM((6, 192, 256), BF16),
+            pltpu.VMEM((6, 192, 256), BF16),
+            pltpu.VMEM((2, 192, 256), F32),
             pltpu.VMEM((4, 192, 128), BF16),
             pltpu.VMEM((4, 192, 128), BF16),
         ] + dma,

time: 59.9 us -> 57.7 us (0.963)
  Pallas kernels: 58.1 us -> 56 us
    pallas_call x1, Pallas kernels: 58.1 us -> 56 us  [body(): pl.pallas_call(kernel, out_shape=jax.ShapeDtypeStruct((HS, HEADS * HS), B...]
where the time goes in v4:
time: 57.7 us; the launch traced here: 57.5 us
  Pallas kernels  56 us (97%)
  local copies, waits for them, and re-layouts  1.54 us (3%)
    pallas_call x1, Pallas kernels, body(): pl.pallas_call(kernel, out_shape=jax.ShapeDtypeStruct((HS, HEADS * HS), B...  56 us
    unnamed x1, local copies, waits for them, and re-layouts  1.54 us

profile of v4, /device:TPU:1, one launch (start us, length us, event | category | flops | bytes accessed | tf_op | source)
XLA Modules:
  0.0 57.5 jit_solution(9662769363166763804)
XLA Ops:
  0.0 56.0 %shard_map.55 = bf16[128,384]{1,0:T(8,128)(2,1)} custom-call(bf16[128,384]{1,0:T(8,128)(2,1)} %q_ref.1, bf16[128,384]{1,0:T(8,128)(2,1)} %k_ref.1, bf16[128,384]{1,0:T(8,128)(2,1)} %v_ref.1, f32[384]{0:T(512)} %g_ref.1, bf16[192,384]{1,0:T(8,128)(2,1)} %bitcast.1), custom_call_target="tpu_custom_call" | custom-call | tf_op jit(solution)/shard_map/pallas_call | solution.py:306
  56.0 1.5 %copy.7 = bf16[128,384]{1,0:T(8,128)(2,1)} copy(bf16[128,384]{1,0:T(8,128)(2,1)} %shard_map.55) | data formatting | bytes 196608

commit v5 on v4

--- a/solution.py
+++ b/solution.py
@@ -51,50 +51,6 @@
             for way in (0, 1):
                 for sub in self.subs(way, step):
                     self.copy(way, step, sub, step - 1).wait_send()
-
-
-class Line:
-    def __init__(self, buf, pos, device, send, recv):
-        self.buf, self.pos, self.device, self.send, self.recv = buf, pos, device, send, recv
-        self.half = buf.shape[1] // 2
-
-    def copy(self, way, step, sub, back):
-        origin = lax.rem(self.pos + (4 - back if way == 0 else back), 4)
-        ref = self.buf.at[origin, pl.ds(sub * self.half, self.half)]
-        i = way * 6 + (step - 1) * 2 + sub
-        return remote(ref, ref, self.send.at[i], self.recv.at[i], self.device(way))
-
-    def room(self, way):
-        return self.pos if way == 0 else 3 - self.pos
-
-    def sends(self, way, step):
-        return jnp.logical_and(self.room(way) < 3, self.room(way) >= step - 1)
-
-    def start(self):
-        for sub in (0, 1):
-            for way in (0, 1):
-                @pl.when(self.sends(way, 1))
-                def _():
-                    self.copy(way, 1, sub, 0).start()
-
-    def hop(self, step):
-        for sub in (0, 1):
-            for way in (0, 1):
-                @pl.when(self.room(way) >= step)
-                def _():
-                    self.copy(way, step, sub, step).wait_recv()
-                if step < 3:
-                    @pl.when(self.sends(way, step + 1))
-                    def _():
-                        self.copy(way, step + 1, sub, step).start()
-
-    def finish(self):
-        for step in (1, 2, 3):
-            for way in (0, 1):
-                for sub in (0, 1):
-                    @pl.when(self.sends(way, step))
-                    def _():
-                        self.copy(way, step, sub, step - 1).wait_send()
 
 
 def nt(a, b):
@@ -206,13 +162,15 @@
         scale = lax.rsqrt(jnp.mean(mixed * mixed, axis=-1, keepdims=True) + 1e-06)
         att[yl, :, cols] = (mixed * scale * g_ref[cols]).astype(BF16)
 
-    a_line = Line(att, yl, lambda way: dev(yl=lax.rem(yl + (1 if way == 0 else 3), 4)), as_, ar)
-    a_line.start()
+    def copy_a(d, to, frm):
+        return remote(att.at[frm], att.at[frm], as_.at[d - 1], ar.at[d - 1], dev(yl=to))
+
+    for d in (2, 1, 3):
+        copy_a(d, lax.rem(yl + d, 4), yl).start()
     w_ring.hop(3)
-    a_line.hop(1)
-    a_line.hop(2)
     w_ring.hop(4)
-    a_line.hop(3)
+    for d in (1, 2, 3):
+        copy_a(d, lax.rem(yl + d, 4), lax.rem(yl + 4 - d, 4)).wait_recv()
 
     def tokens(half):
         return att[pl.ds(2 * half, 2)].reshape(2 * HS, HEADS * HS)
@@ -236,7 +194,7 @@
         pc_out[e * 4 + i - 1] = unit(e, i, theirs).astype(BF16)
         copy_c(e, i).start()
 
-    order = [(e, i) for e in (1, 0) for i in (2, 1, 3, 4)]
+    order = [(e, i) for e in (1, 0) for i in (1, 3, 2, 4)]
     give(*order[0])
     for n, (e, i) in enumerate(order):
         if n < 7:
@@ -294,7 +252,8 @@
             copy2(d, lax.rem(z + d, 8)).wait_send()
 
     w_ring.finish()
-    a_line.finish()
+    for d in (1, 2, 3):
+        copy_a(d, lax.rem(yl + d, 4), yl).wait_send()
     for i in (1, 2, 3, 4):
         copy_c(0, i).wait_send()
         copy_c(1, i).wait_send()
@@ -302,7 +261,7 @@
 
 
 def body(queries, keys, values, norm_gain, out_weight):
-    dma = [pltpu.SemaphoreType.DMA((n,)) for n in (3, 7, 3, 16, 12, 8, 6, 4) for _ in (0, 1)]
+    dma = [pltpu.SemaphoreType.DMA((n,)) for n in (3, 7, 3, 16, 3, 8, 6, 4) for _ in (0, 1)]
     return pl.pallas_call(
         kernel,
         out_shape=jax.ShapeDtypeStruct((HS, HEADS * HS), BF16),

time: 57.7 us -> 56.8 us (0.984)
  Pallas kernels: 56 us -> 55.1 us
    pallas_call x1, Pallas kernels: 56 us -> 55.1 us  [body(): pl.pallas_call(kernel, out_shape=jax.ShapeDtypeStruct((HS, HEADS * HS), B...]
where the time goes in v5:
time: 56.8 us; the launch traced here: 56.7 us
  Pallas kernels  55.1 us (97%)
  local copies, waits for them, and re-layouts  1.54 us (3%)
    pallas_call x1, Pallas kernels, body(): pl.pallas_call(kernel, out_shape=jax.ShapeDtypeStruct((HS, HEADS * HS), B...  55.1 us
    unnamed x1, local copies, waits for them, and re-layouts  1.54 us

profile of v5, /device:TPU:1, one launch (start us, length us, event | category | flops | bytes accessed | tf_op | source)
XLA Modules:
  0.0 56.7 jit_solution(14923999402843828704)
XLA Ops:
  0.0 55.1 %shard_map.55 = bf16[128,384]{1,0:T(8,128)(2,1)} custom-call(bf16[128,384]{1,0:T(8,128)(2,1)} %q_ref.1, bf16[128,384]{1,0:T(8,128)(2,1)} %k_ref.1, bf16[128,384]{1,0:T(8,128)(2,1)} %v_ref.1, f32[384]{0:T(512)} %g_ref.1, bf16[192,384]{1,0:T(8,128)(2,1)} %bitcast.1), custom_call_target="tpu_custom_call" | custom-call | tf_op jit(solution)/shard_map/pallas_call | solution.py:265
  55.1 1.5 %copy.7 = bf16[128,384]{1,0:T(8,128)(2,1)} copy(bf16[128,384]{1,0:T(8,128)(2,1)} %shard_map.55) | data formatting | bytes 196608
